TPU v7x, 256 devices: a whole 4x4x8 slice. The times are simulated.
256 devices in a mesh: dp: 32 (over z, x_lo, core), tp: 8 (over x_hi, y).
Axes of the slice: x: 4 (x_hi: 2, x_lo: 2; x = x_hi * 2 + x_lo), y: 4, z: 8, core: 2. Of those that a mesh axis runs over, the one named last changes fastest.
Arguments:
- queries: bfloat16 [256, 8192], P('dp', 'tp'), may hold values from -5 to 5
- prefix_kv: bfloat16 [2, 65536, 1024], P(None, 'dp', 'tp'), may hold values from -5 to 5
- cache_kv: bfloat16 [2, 2048, 64, 1024], P(None, 'dp', None, 'tp'), may hold values from -5 to 5
- lengths: int32 [256], P('dp'), may hold values from 1 to 512, as said below
- page_table: int32 [32, 64], P('dp'), may hold values from 0 to 63, each once within a row
- owner: int32 [32], replicated, may hold values from 0 to 31, as said below
- readers: int32 [16], replicated, may hold values from 0 to 31, as said below
- w_out: bfloat16 [8192, 4096], P('tp'), may hold values from -0.5 to 0.5
Outputs:
- projected: bfloat16 [256, 4096], P('dp', 'tp')
Inputs may be any that keep to these rules, and one draw needn't show every extreme that they name: `lengths`: at most 512, reached by some request in every draw. `page_table`: each row holds every page id of its replica once. `owner`: every replica index once. `readers`: 16 distinct replica indices, none of them owner[0].
All inputs are finite; a program needn't handle non-finite values.
Results may differ from a plain program's by a relative error of at most 0.0051.
Values may be sent and summed in bfloat16 or wider, within the bound.
A program may use at most 64 MiB of HBM per device.

v0:
```python
import functools
import math

import jax
import jax.numpy as jnp
from jax import lax
from jax.experimental import pallas as pl
from jax.experimental.pallas import tpu as pltpu
from jax.sharding import PartitionSpec as P

HD = 128
MESH = pl.DeviceIdType.MESH
LOG2E = math.log2(math.e)
LOW = -1e30
NZ, NX, NC, NY, NXH = 8, 2, 2, 4, 2
TP_STEPS = sorted(
    [(kx, ky) for kx in range(NXH) for ky in range(NY) if kx or ky],
    key=lambda k: -(2 * k[0] + min(k[1], NY - k[1])),
)


def nt_dot(a, b):
    return lax.dot_general(
        a, b, (((1,), (1,)), ((), ())), preferred_element_type=jnp.float32
    )


def kernel(
    oz,
    ox,
    lens_ref,
    table_ref,
    owner_ref,
    readers_ref,
    q_hbm,
    prefix_hbm,
    cache_hbm,
    w_hbm,
    out_ref,
    q_in,
    q_f32,
    q_rows,
    cache,
    kv,
    w,
    q_buf,
    o_send,
    s_send,
    o_recv,
    s_recv,
    num_res,
    ml_res,
    attn_f32,
    lse_f32,
    part_send,
    part_recv,
    local_sem,
    kv_send,
    kv_recv,
    q_send_sem,
    q_recv_sem,
    o_send_sem,
    s_send_sem,
    o_recv_sem,
    s_recv_sem,
    p_send_sem,
    p_recv_sem,
):
    dp, tp = lax.axis_index("dp"), lax.axis_index("tp")
    z, x, c = dp // 4, (dp // 2) % 2, dp % 2
    xh, y = tp // NY, tp % NY
    dz, dx = (z + NZ - oz) % NZ, (x + NX - ox) % NX
    here = dz * 2 + dx
    at_owner = here == 0
    rows = q_in.shape[0]
    heads = q_in.shape[1] // HD
    n = rows * heads
    pages, page = cache.shape[1], cache.shape[2]
    per = pages // rows
    c2 = LOG2E / HD**0.5

    def at(zz, xx, cc):
        return (zz * 4 + xx * 2 + cc, tp)

    def tp_peer(kx, ky):
        return (dp, ((xh + kx) % NXH) * NY + (y + ky) % NY)

    barrier = pltpu.get_barrier_semaphore()
    for k in TP_STEPS:
        pl.semaphore_signal(barrier, 1, device_id=tp_peer(*k), device_id_type=MESH)

    @pl.when(at_owner)
    def _():
        pl.semaphore_signal(barrier, 1, device_id=at(oz, ox, 1 - c), device_id_type=MESH)
        for i in range(2 * NZ - 1, 0, -1):
            pl.semaphore_signal(
                barrier,
                1,
                device_id=at((oz + i // 2) % NZ, (ox + i % 2) % NX, c),
                device_id_type=MESH,
            )

    load_q = pltpu.make_async_copy(q_hbm, q_in, local_sem.at[0])
    load_cache = pltpu.make_async_copy(cache_hbm, cache, local_sem.at[1])
    load_w = pltpu.make_async_copy(w_hbm, w, local_sem.at[2])
    load_kv = pltpu.make_async_copy(prefix_hbm, kv.at[0], local_sem.at[3])
    load_q.start()
    load_cache.start()

    @pl.when(at_owner)
    def _():
        load_kv.start()

    load_w.start()

    load_q.wait()
    for g in range(heads):
        q_f32[pl.ds(g, rows, stride=heads), :] = q_in[:, g * HD : (g + 1) * HD].astype(
            jnp.float32
        )
    q_rows[...] = q_f32[...].astype(jnp.bfloat16)

    def query_copy():
        return pltpu.make_async_remote_copy(
            q_rows,
            q_buf.at[dz, pl.ds(pl.multiple_of(dx * n, n), n)],
            q_send_sem,
            q_recv_sem.at[here],
            device_id=at(oz, ox, c),
            device_id_type=MESH,
        )

    @pl.when(jnp.logical_not(at_owner))
    def _():
        pl.semaphore_wait(barrier, len(TP_STEPS) + 1)
        query_copy().start()

    def kv_copy(i):
        return pltpu.make_async_remote_copy(
            prefix_hbm.at[i],
            kv.at[1, i],
            kv_send.at[i],
            kv_recv.at[i],
            device_id=at(oz, ox, 1 - c),
            device_id_type=MESH,
        )

    load_cache.wait()
    def resident(b, carry):
        mine = pl.ds(pl.multiple_of(b * heads, heads), heads)
        keys = jnp.concatenate(
            [cache[0, table_ref[0, b * per + j]] for j in range(per)], axis=0
        )
        s = nt_dot(q_f32[mine, :].astype(jnp.bfloat16), keys)
        pos = lax.broadcasted_iota(jnp.int32, s.shape, 1)
        s = jnp.where(pos < lens_ref[b], s, LOW)
        m = jnp.max(s, axis=-1, keepdims=True)
        e = jnp.exp2((s - m) * c2)
        values = jnp.concatenate(
            [cache[1, table_ref[0, b * per + j]] for j in range(per)], axis=0
        )
        ml_res[0, mine, :] = jnp.broadcast_to(m * c2, (heads, HD))
        ml_res[1, mine, :] = jnp.broadcast_to(
            jnp.sum(e, axis=-1, keepdims=True), (heads, HD)
        )
        num_res[mine, :] = jnp.dot(
            e.astype(jnp.bfloat16), values, preferred_element_type=jnp.float32
        )
        return carry

    lax.fori_loop(0, rows, resident, 0)

    @pl.when(at_owner)
    def _():
        pl.semaphore_wait(barrier, len(TP_STEPS) + 1)
        for i in range(2):
            kv_copy(i).start()
        q_buf[0, 0:n, :] = q_rows[...]
        load_kv.wait()
        for i in range(2):
            kv_copy(i).wait()
        source = (owner_ref[0] % NC + c) % 2

        def reply(zz, k, i):
            peer = at((oz + zz) % NZ, (ox + k) % NX, c)
            return (
                pltpu.make_async_remote_copy(
                    o_send.at[zz, pl.ds(k * n, n)],
                    o_recv,
                    o_send_sem.at[i],
                    o_recv_sem,
                    device_id=peer,
                    device_id_type=MESH,
                ),
                pltpu.make_async_remote_copy(
                    s_send.at[zz],
                    s_recv,
                    s_send_sem.at[i],
                    s_recv_sem,
                    device_id=peer,
                    device_id_type=MESH,
                ),
            )

        def arrival(zz, k):
            return pltpu.make_async_remote_copy(
                q_rows,
                q_buf.at[zz, pl.ds(k * n, n)],
                q_send_sem,
                q_recv_sem.at[zz * 2 + k],
                device_id=at(oz, ox, 1 - c),
                device_id_type=MESH,
            )

        def serve(t, carry):
            far = (t + 1) // 2
            zz = (t % 2) * far + (1 - t % 2) * ((NZ - far) % NZ)

            @pl.when(t > 0)
            def _():
                arrival(zz, 0).wait_recv()

            arrival(zz, 1).wait_recv()
            s = nt_dot(q_buf[zz], kv[source, 0])
            m = jnp.max(s, axis=-1, keepdims=True)
            e = jnp.exp2((s - m) * c2)
            total = jnp.sum(e, axis=-1, keepdims=True)
            num = jnp.dot(
                e.astype(jnp.bfloat16), kv[source, 1], preferred_element_type=jnp.float32
            )
            o_send[zz] = (num / total).astype(jnp.bfloat16)
            lse = m * c2 + jnp.log(total) * LOG2E
            s_send[zz] = jnp.transpose(jnp.broadcast_to(lse, (2 * n, HD)))[0:8, :]

            @pl.when(t > 0)
            def _():
                for copy in reply(zz, 0, zz * 2):
                    copy.start()

            for copy in reply(zz, 1, zz * 2 + 1):
                copy.start()
            return carry

        lax.fori_loop(0, NZ, serve, 0)
        o_recv[...] = o_send[0, 0:n, :]
        s_recv[...] = s_send[0]

        def settle(i, carry):
            for copy in reply(0, 0, i):
                copy.wait_send()
            return carry

        lax.fori_loop(1, 2 * NZ, settle, 0)

    @pl.when(jnp.logical_not(at_owner))
    def _():
        query_copy().wait_send()
        pltpu.make_async_remote_copy(
            o_recv, o_recv, o_send_sem.at[0], o_recv_sem, device_id=at(oz, ox, c), device_id_type=MESH
        ).wait_recv()
        pltpu.make_async_remote_copy(
            s_recv, s_recv, s_send_sem.at[0], s_recv_sem, device_id=at(oz, ox, c), device_id_type=MESH
        ).wait_recv()

    reads = readers_ref[0] == dp
    for i in range(1, readers_ref.shape[0]):
        reads = jnp.logical_or(reads, readers_ref[i] == dp)
    lse_f32[...] = jnp.transpose(jnp.broadcast_to(s_recv[0:1, :], (HD, HD)))
    lse = lse_f32[pl.ds(pl.multiple_of(dx * n, n), n), :]
    lse = jnp.where(reads, lse, LOW)
    m_res, l_res = ml_res[0], ml_res[1]
    top = jnp.maximum(m_res, lse)
    w_res, w_pre = jnp.exp2(m_res - top), jnp.exp2(lse - top)
    attn_f32[...] = (num_res[...] * w_res + o_recv[...].astype(jnp.float32) * w_pre) / (
        l_res * w_res + w_pre
    )
    attn = jnp.concatenate(
        [attn_f32[pl.ds(g, rows, stride=heads), :] for g in range(heads)], axis=1
    ).astype(jnp.bfloat16)

    load_w.wait()
    cols = out_ref.shape[1]

    def block(kx, ky):
        start = (((xh + kx) % NXH) * NY + (y + ky) % NY) * cols
        return jnp.dot(
            attn,
            w[:, pl.ds(pl.multiple_of(start, cols), cols)],
            preferred_element_type=jnp.float32,
        )

    def part_copy(kx, ky):
        i = kx * NY + ky
        return pltpu.make_async_remote_copy(
            part_send.at[i],
            part_recv.at[i],
            p_send_sem.at[i],
            p_recv_sem.at[i],
            device_id=tp_peer(kx, ky),
            device_id_type=MESH,
        )

    def project(i, carry):
        k = NXH * NY - 1 - i
        kx, ky = k // NY, k % NY
        part_send[k] = block(kx, ky)

        @pl.when(k > 0)
        def _():
            part_copy(kx, ky).start()

        return carry

    lax.fori_loop(0, NXH * NY, project, 0)
    total = part_send[0]
    for k in range(NXH * NY - 1, 0, -1):
        part_copy(k // NY, k % NY).wait_recv()
        total = total + part_recv[k]
    out_ref[...] = total.astype(out_ref.dtype)
    for k in range(1, NXH * NY):
        part_copy(k // NY, k % NY).wait_send()


def attend(place, q, prefix, cache, lengths, table, owner, readers, w_out):
    rows, width = q.shape
    n = rows * width // HD
    cols = w_out.shape[1] // (NXH * NY)
    keys = prefix.shape[1]
    bf16, f32 = jnp.bfloat16, jnp.float32
    dma = pltpu.SemaphoreType.DMA
    smem = pl.BlockSpec(memory_space=pltpu.SMEM)
    whole = pl.BlockSpec(memory_space=pl.ANY)
    return pl.pallas_call(
        functools.partial(kernel, place // NX, place % NX),
        out_shape=jax.ShapeDtypeStruct((rows, cols), bf16),
        in_specs=[smem] * 4 + [whole] * 4,
        out_specs=pl.BlockSpec(memory_space=pltpu.VMEM),
        scratch_shapes=[
            pltpu.VMEM((rows, width), bf16),
            pltpu.VMEM((n, HD), f32),
            pltpu.VMEM((n, HD), bf16),
            pltpu.VMEM(cache.shape, bf16),
            pltpu.VMEM((2, 2, keys, HD), bf16),
            pltpu.VMEM(w_out.shape, bf16),
            pltpu.VMEM((NZ, 2 * n, HD), bf16),
            pltpu.VMEM((NZ, 2 * n, HD), bf16),
            pltpu.VMEM((NZ, 8, HD), f32),
            pltpu.VMEM((n, HD), bf16),
            pltpu.VMEM((8, HD), f32),
            pltpu.VMEM((n, HD), f32),
            pltpu.VMEM((2, n, HD), f32),
            pltpu.VMEM((n, HD), f32),
            pltpu.VMEM((HD, HD), f32),
            pltpu.VMEM((NXH * NY, rows, cols), f32),
            pltpu.VMEM((NXH * NY, rows, cols), f32),
            dma((4,)),
            dma((2,)),
            dma((2,)),
            dma,
            dma((2 * NZ,)),
            dma((2 * NZ,)),
            dma((2 * NZ,)),
            dma,
            dma,
            dma((NXH * NY,)),
            dma((NXH * NY,)),
        ],
        compiler_params=pltpu.CompilerParams(
            collective_id=place, has_side_effects=True, vmem_limit_bytes=48 << 20
        ),
        name=f"attend_{place}",
    )(lengths, table, owner, readers, q, prefix, cache, w_out)


def shards(queries, prefix_kv, cache_kv, lengths, page_table, owner, readers, w_out):
    return lax.switch(
        owner[0] // NC,
        [functools.partial(attend, place) for place in range(NZ * NX)],
        queries,
        prefix_kv,
        cache_kv,
        lengths,
        page_table,
        owner,
        readers,
        w_out,
    )


def solution(mesh):
    placed = (
        P("dp", "tp"),
        P(None, "dp", "tp"),
        P(None, "dp", None, "tp"),
        P("dp"),
        P("dp", None),
        P(),
        P(),
        P("tp", None),
    )
    return jax.shard_map(
        shards, mesh=mesh, in_specs=placed, out_specs=P("dp", "tp"), check_vma=False
    )
```

profile of v0, /device:TPU:64, one launch (start us, length us, event | category | flops | bytes accessed | tf_op | source)
XLA Modules:
  0.0 34.8 jit_solution(3264761842832445772)
XLA Ops:
  2.6 31.6 %conditional.1 = (bf16[8,512]{1,0:T(8,128)(2,1)S(1)}) conditional(s32[]{:T(128)} %clamp.3, (s32[8]{0:T(128)}, s32[1,64]{1,0:T(1,128)}, s32[32]{0:T(128)}, s32[16]{0:T(128)}, bf16[8,1024]{1,0:T(8,128)(2,1)}, /*index=5*/bf16[2,2048,128]{2,1,0:T(8,128)(2,1)}, bf16[2,64,64,128]{3,2,1,0:T(8,128)(2,1)}, ...), branch_computations={%region_0.1_spmd, %region_1.2_spmd, %region_2.3_spmd, %region_3.4_... | conditional | bytes 8 | solution.py:376
  2.9 31.1 %attend_13.1 = bf16[8,512]{1,0:T(8,128)(2,1)S(1)} custom-call(s32[8]{0:T(128)} %get-tuple-element.382.lens_ref, s32[1,64]{1,0:T(1,128)} %get-tuple-element.383.table_ref, s32[32]{0:T(128)} %get-tuple-element.384.owner_ref, s32[16]{0:T(128)} %get-tuple-element.385.readers_ref, bf16[8,1024]{1,0:T(8,128)(2,1)} %get-tuple-element.386.q_hbm, ...), custom_call_target="tpu_custom_call" | custom-call | tf_op jit(solution)/shard_map/cond/branch_13_fun/attend_13/pallas_call | solution.py:333
  34.2 0.6 %copy.42 = bf16[8,512]{1,0:T(8,128)(2,1)} copy(bf16[8,512]{1,0:T(8,128)(2,1)S(1)} %get-tuple-element.406) | data formatting | bytes 16384
where the time goes:
time: 35 us; the launch traced here: 34.8 us
  Pallas kernels  31.1 us (89%)
  between operations  2.62 us (7%)
  local copies, waits for them, and re-layouts  0.6 us (2%)
  loops' own time  0.54 us (2%)
    pallas_call x1, Pallas kernels, attend(): pl.pallas_call(functools.partial(kernel, place // NX, place % NX), out_sh...  31.1 us

commit v1 on v0

--- a/solution.py
+++ b/solution.py
@@ -65,6 +65,8 @@
     s_recv_sem,
     p_send_sem,
     p_recv_sem,
+    known,
+    clear,
 ):
     dp, tp = lax.axis_index("dp"), lax.axis_index("tp")
     z, x, c = dp // 4, (dp // 2) % 2, dp % 2
@@ -86,8 +88,11 @@
         return (dp, ((xh + kx) % NXH) * NY + (y + ky) % NY)
 
     barrier = pltpu.get_barrier_semaphore()
-    for k in TP_STEPS:
-        pl.semaphore_signal(barrier, 1, device_id=tp_peer(*k), device_id_type=MESH)
+    beside = here == 1
+
+    def greet_tp(sem):
+        for k in TP_STEPS:
+            pl.semaphore_signal(sem, 1, device_id=tp_peer(*k), device_id_type=MESH)
 
     @pl.when(at_owner)
     def _():
@@ -100,17 +105,35 @@
                 device_id_type=MESH,
             )
 
+    @pl.when(jnp.logical_not(at_owner))
+    def _():
+        greet_tp(barrier)
+
     load_q = pltpu.make_async_copy(q_hbm, q_in, local_sem.at[0])
     load_cache = pltpu.make_async_copy(cache_hbm, cache, local_sem.at[1])
     load_w = pltpu.make_async_copy(w_hbm, w, local_sem.at[2])
     load_kv = pltpu.make_async_copy(prefix_hbm, kv.at[0], local_sem.at[3])
+
+    def kv_copy(i):
+        return pltpu.make_async_remote_copy(
+            prefix_hbm.at[i],
+            kv.at[1, i],
+            kv_send.at[i],
+            kv_recv.at[i],
+            device_id=at(oz, ox, 1 - c),
+            device_id_type=MESH,
+        )
+
     load_q.start()
+
+    @pl.when(at_owner)
+    def _():
+        load_kv.start()
+        pl.semaphore_wait(barrier, 1)
+        for i in range(2):
+            kv_copy(i).start()
+
     load_cache.start()
-
-    @pl.when(at_owner)
-    def _():
-        load_kv.start()
-
     load_w.start()
 
     load_q.wait()
@@ -135,17 +158,14 @@
         pl.semaphore_wait(barrier, len(TP_STEPS) + 1)
         query_copy().start()
 
-    def kv_copy(i):
-        return pltpu.make_async_remote_copy(
-            prefix_hbm.at[i],
-            kv.at[1, i],
-            kv_send.at[i],
-            kv_recv.at[i],
-            device_id=at(oz, ox, 1 - c),
-            device_id_type=MESH,
-        )
+        @pl.when(beside)
+        def _():
+            greet_tp(known)
+            pl.semaphore_wait(known, len(TP_STEPS))
+            pl.semaphore_signal(clear, 1, device_id=at(oz, ox, c), device_id_type=MESH)
 
     load_cache.wait()
+
     def resident(b, carry):
         mine = pl.ds(pl.multiple_of(b * heads, heads), heads)
         keys = jnp.concatenate(
@@ -172,9 +192,6 @@
 
     @pl.when(at_owner)
     def _():
-        pl.semaphore_wait(barrier, len(TP_STEPS) + 1)
-        for i in range(2):
-            kv_copy(i).start()
         q_buf[0, 0:n, :] = q_rows[...]
         load_kv.wait()
         for i in range(2):
@@ -251,6 +268,7 @@
             return carry
 
         lax.fori_loop(1, 2 * NZ, settle, 0)
+        pl.semaphore_wait(clear, 1)
 
     @pl.when(jnp.logical_not(at_owner))
     def _():
@@ -364,6 +382,8 @@
             dma,
             dma((NXH * NY,)),
             dma((NXH * NY,)),
+            pltpu.SemaphoreType.REGULAR,
+            pltpu.SemaphoreType.REGULAR,
         ],
         compiler_params=pltpu.CompilerParams(
             collective_id=place, has_side_effects=True, vmem_limit_bytes=48 << 20
@@ -374,7 +394,7 @@
 
 def shards(queries, prefix_kv, cache_kv, lengths, page_table, owner, readers, w_out):
     return lax.switch(
-        owner[0] // NC,
+        lax.shift_right_logical(owner[0], 1),
         [functools.partial(attend, place) for place in range(NZ * NX)],
         queries,
         prefix_kv,

time: 35 us -> 30.7 us (0.88)
  Pallas kernels: 31.1 us -> 29 us
  between operations: 2.62 us -> 0.66 us
    pallas_call x1, Pallas kernels: 31.1 us -> 29 us  [attend(): pl.pallas_call(functools.partial(kernel, place // NX, place % NX), out_sh...]
where the time goes in v1:
time: 30.7 us; the launch traced here: 30.5 us
  Pallas kernels  29 us (94%)
  between operations  0.66 us (2%)
  local copies, waits for them, and re-layouts  0.6 us (2%)
    pallas_call x1, Pallas kernels, attend(): pl.pallas_call(functools.partial(kernel, place // NX, place % NX), out_sh...  29 us

profile of v1, /device:TPU:64, one launch (start us, length us, event | category | flops | bytes accessed | tf_op | source)
XLA Modules:
  0.0 30.5 jit_solution(8482977237490487876)
XLA Ops:
  0.7 29.3 %conditional.1 = (bf16[8,512]{1,0:T(8,128)(2,1)S(1)}) conditional(s32[]{:T(128)} %bitcast, (s32[8]{0:T(128)}, s32[1,64]{1,0:T(1,128)}, s32[32]{0:T(128)}, s32[16]{0:T(128)}, bf16[8,1024]{1,0:T(8,128)(2,1)}, /*index=5*/bf16[2,2048,128]{2,1,0:T(8,128)(2,1)}, bf16[2,64,64,128]{3,2,1,0:T(8,128)(2,1)}, ...), branch_computations={%region_0.0_spmd, %region_1.0_spmd, %region_2.0_spmd, %region_3.0_... | conditional | bytes 8 | solution.py:396
  0.9 29.0 %attend_12.1 = bf16[8,512]{1,0:T(8,128)(2,1)S(1)} custom-call(s32[8]{0:T(128)} %get-tuple-element.374.lens_ref, s32[1,64]{1,0:T(1,128)} %get-tuple-element.375.table_ref, s32[32]{0:T(128)} %get-tuple-element.376.owner_ref, s32[16]{0:T(128)} %get-tuple-element.377.readers_ref, bf16[8,1024]{1,0:T(8,128)(2,1)} %get-tuple-element.378.q_hbm, ...), custom_call_target="tpu_custom_call" | custom-call | tf_op jit(solution)/shard_map/cond/branch_12_fun/attend_12/pallas_call | solution.py:351
  29.9 0.6 %copy.42 = bf16[8,512]{1,0:T(8,128)(2,1)} copy(bf16[8,512]{1,0:T(8,128)(2,1)S(1)} %get-tuple-element.406) | data formatting | bytes 16384

commit v2 on v1

--- a/solution.py
+++ b/solution.py
@@ -28,15 +28,19 @@
 def kernel(
     oz,
     ox,
-    lens_ref,
-    table_ref,
-    owner_ref,
-    readers_ref,
+    lens_hbm,
+    table_hbm,
+    owner_hbm,
+    readers_hbm,
     q_hbm,
     prefix_hbm,
     cache_hbm,
     w_hbm,
     out_ref,
+    lens_ref,
+    table_ref,
+    owner_ref,
+    readers_ref,
     q_in,
     q_f32,
     q_rows,
@@ -124,7 +128,18 @@
             device_id_type=MESH,
         )
 
+    load_scalars = [
+        pltpu.make_async_copy(src, dst, local_sem.at[4 + i])
+        for i, (src, dst) in enumerate(
+            zip(
+                (lens_hbm, table_hbm, owner_hbm, readers_hbm),
+                (lens_ref, table_ref, owner_ref, readers_ref),
+            )
+        )
+    ]
     load_q.start()
+    for copy in load_scalars:
+        copy.start()
 
     @pl.when(at_owner)
     def _():
@@ -146,7 +161,7 @@
     def query_copy():
         return pltpu.make_async_remote_copy(
             q_rows,
-            q_buf.at[dz, pl.ds(pl.multiple_of(dx * n, n), n)],
+            q_buf.at[here],
             q_send_sem,
             q_recv_sem.at[here],
             device_id=at(oz, ox, c),
@@ -164,6 +179,8 @@
             pl.semaphore_wait(known, len(TP_STEPS))
             pl.semaphore_signal(clear, 1, device_id=at(oz, ox, c), device_id_type=MESH)
 
+    for copy in load_scalars:
+        copy.wait()
     load_cache.wait()
 
     def resident(b, carry):
@@ -192,92 +209,100 @@
 
     @pl.when(at_owner)
     def _():
-        q_buf[0, 0:n, :] = q_rows[...]
+        q_buf[0] = q_rows[...]
         load_kv.wait()
         for i in range(2):
             kv_copy(i).wait()
         source = (owner_ref[0] % NC + c) % 2
 
-        def reply(zz, k, i):
-            peer = at((oz + zz) % NZ, (ox + k) % NX, c)
+        def reply(i):
+            peer = at((oz + i // 2) % NZ, (ox + i % 2) % NX, c)
             return (
                 pltpu.make_async_remote_copy(
-                    o_send.at[zz, pl.ds(k * n, n)],
+                    o_send.at[i],
                     o_recv,
-                    o_send_sem.at[i],
+                    o_send_sem,
                     o_recv_sem,
                     device_id=peer,
                     device_id_type=MESH,
                 ),
                 pltpu.make_async_remote_copy(
-                    s_send.at[zz],
+                    s_send.at[i],
                     s_recv,
-                    s_send_sem.at[i],
+                    s_send_sem,
                     s_recv_sem,
                     device_id=peer,
                     device_id_type=MESH,
                 ),
             )
 
-        def arrival(zz, k):
+        def arrival(i):
             return pltpu.make_async_remote_copy(
                 q_rows,
-                q_buf.at[zz, pl.ds(k * n, n)],
+                q_buf.at[i],
                 q_send_sem,
-                q_recv_sem.at[zz * 2 + k],
+                q_recv_sem.at[i],
                 device_id=at(oz, ox, 1 - c),
                 device_id_type=MESH,
             )
 
-        def serve(t, carry):
-            far = (t + 1) // 2
-            zz = (t % 2) * far + (1 - t % 2) * ((NZ - far) % NZ)
-
-            @pl.when(t > 0)
+        def serve(step, carry):
+            za = (step + 1) % 4
+            own = 1 - (za + 3) // 4
+            zb = NZ - za - 4 * own
+            ids = (za * 2, za * 2 + 1, zb * 2, zb * 2 + 1)
+
+            @pl.when(own == 0)
             def _():
-                arrival(zz, 0).wait_recv()
-
-            arrival(zz, 1).wait_recv()
-            s = nt_dot(q_buf[zz], kv[source, 0])
+                arrival(ids[0]).wait_recv()
+
+            for i in ids[1:]:
+                arrival(i).wait_recv()
+            q = jnp.concatenate([q_buf[i] for i in ids], axis=0)
+            s = nt_dot(q, kv[source, 0])
             m = jnp.max(s, axis=-1, keepdims=True)
             e = jnp.exp2((s - m) * c2)
             total = jnp.sum(e, axis=-1, keepdims=True)
             num = jnp.dot(
                 e.astype(jnp.bfloat16), kv[source, 1], preferred_element_type=jnp.float32
             )
-            o_send[zz] = (num / total).astype(jnp.bfloat16)
-            lse = m * c2 + jnp.log(total) * LOG2E
-            s_send[zz] = jnp.transpose(jnp.broadcast_to(lse, (2 * n, HD)))[0:8, :]
-
-            @pl.when(t > 0)
+            o = (num / total).astype(jnp.bfloat16)
+            lse = jnp.broadcast_to(m * c2 + jnp.log(total) * LOG2E, (4 * n, HD))
+            for j in range(2):
+                row = jnp.transpose(lse[2 * n * j : 2 * n * (j + 1)])[0:8, :]
+                s_send[ids[2 * j]] = row
+                s_send[ids[2 * j + 1]] = row
+            for j in range(4):
+                o_send[ids[j]] = o[n * j : n * (j + 1)]
+            for i in ids[:0:-1]:
+                for copy in reply(i):
+                    copy.start()
+
+            @pl.when(own == 0)
             def _():
-                for copy in reply(zz, 0, zz * 2):
+                for copy in reply(ids[0]):
                     copy.start()
 
-            for copy in reply(zz, 1, zz * 2 + 1):
-                copy.start()
             return carry
 
-        lax.fori_loop(0, NZ, serve, 0)
-        o_recv[...] = o_send[0, 0:n, :]
+        lax.fori_loop(0, NZ // 2, serve, 0)
+        o_recv[...] = o_send[0]
         s_recv[...] = s_send[0]
-
-        def settle(i, carry):
-            for copy in reply(0, 0, i):
-                copy.wait_send()
-            return carry
-
-        lax.fori_loop(1, 2 * NZ, settle, 0)
+        for ref, sem in ((o_send, o_send_sem), (s_send, s_send_sem)):
+            sent = ref.at[pl.ds(1, 2 * NZ - 1)]
+            pltpu.make_async_remote_copy(
+                sent, sent, sem, sem, device_id=at(oz, ox, 1 - c), device_id_type=MESH
+            ).wait_send()
         pl.semaphore_wait(clear, 1)
 
     @pl.when(jnp.logical_not(at_owner))
     def _():
         query_copy().wait_send()
         pltpu.make_async_remote_copy(
-            o_recv, o_recv, o_send_sem.at[0], o_recv_sem, device_id=at(oz, ox, c), device_id_type=MESH
+            o_recv, o_recv, o_send_sem, o_recv_sem, device_id=at(oz, ox, c), device_id_type=MESH
         ).wait_recv()
         pltpu.make_async_remote_copy(
-            s_recv, s_recv, s_send_sem.at[0], s_recv_sem, device_id=at(oz, ox, c), device_id_type=MESH
+            s_recv, s_recv, s_send_sem, s_recv_sem, device_id=at(oz, ox, c), device_id_type=MESH
         ).wait_recv()
 
     reads = readers_ref[0] == dp
@@ -312,15 +337,15 @@
         return pltpu.make_async_remote_copy(
             part_send.at[i],
             part_recv.at[i],
-            p_send_sem.at[i],
-            p_recv_sem.at[i],
+            p_send_sem,
+            p_recv_sem,
             device_id=tp_peer(kx, ky),
             device_id_type=MESH,
         )
 
     def project(i, carry):
-        k = NXH * NY - 1 - i
-        kx, ky = k // NY, k % NY
+        kx, ky = 1 - i // NY, (i + 2) % NY
+        k = kx * NY + ky
         part_send[k] = block(kx, ky)
 
         @pl.when(k > 0)
@@ -330,13 +355,21 @@
         return carry
 
     lax.fori_loop(0, NXH * NY, project, 0)
+    others = pl.ds(1, NXH * NY - 1)
+    whole = pltpu.make_async_remote_copy(
+        part_send.at[others],
+        part_recv.at[others],
+        p_send_sem,
+        p_recv_sem,
+        device_id=tp_peer(0, 1),
+        device_id_type=MESH,
+    )
+    whole.wait_recv()
     total = part_send[0]
-    for k in range(NXH * NY - 1, 0, -1):
-        part_copy(k // NY, k % NY).wait_recv()
+    for k in range(1, NXH * NY):
         total = total + part_recv[k]
     out_ref[...] = total.astype(out_ref.dtype)
-    for k in range(1, NXH * NY):
-        part_copy(k // NY, k % NY).wait_send()
+    whole.wait_send()
 
 
 def attend(place, q, prefix, cache, lengths, table, owner, readers, w_out):
@@ -346,23 +379,23 @@
     keys = prefix.shape[1]
     bf16, f32 = jnp.bfloat16, jnp.float32
     dma = pltpu.SemaphoreType.DMA
-    smem = pl.BlockSpec(memory_space=pltpu.SMEM)
     whole = pl.BlockSpec(memory_space=pl.ANY)
     return pl.pallas_call(
         functools.partial(kernel, place // NX, place % NX),
         out_shape=jax.ShapeDtypeStruct((rows, cols), bf16),
-        in_specs=[smem] * 4 + [whole] * 4,
+        in_specs=[whole] * 8,
         out_specs=pl.BlockSpec(memory_space=pltpu.VMEM),
         scratch_shapes=[
+            *(pltpu.SMEM(a.shape, a.dtype) for a in (lengths, table, owner, readers)),
             pltpu.VMEM((rows, width), bf16),
             pltpu.VMEM((n, HD), f32),
             pltpu.VMEM((n, HD), bf16),
             pltpu.VMEM(cache.shape, bf16),
             pltpu.VMEM((2, 2, keys, HD), bf16),
             pltpu.VMEM(w_out.shape, bf16),
-            pltpu.VMEM((NZ, 2 * n, HD), bf16),
-            pltpu.VMEM((NZ, 2 * n, HD), bf16),
-            pltpu.VMEM((NZ, 8, HD), f32),
+            pltpu.VMEM((2 * NZ, n, HD), bf16),
+            pltpu.VMEM((2 * NZ, n, HD), bf16),
+            pltpu.VMEM((2 * NZ, 8, HD), f32),
             pltpu.VMEM((n, HD), bf16),
             pltpu.VMEM((8, HD), f32),
             pltpu.VMEM((n, HD), f32),
@@ -371,17 +404,17 @@
             pltpu.VMEM((HD, HD), f32),
             pltpu.VMEM((NXH * NY, rows, cols), f32),
             pltpu.VMEM((NXH * NY, rows, cols), f32),
-            dma((4,)),
+            dma((8,)),
             dma((2,)),
             dma((2,)),
             dma,
             dma((2 * NZ,)),
-            dma((2 * NZ,)),
-            dma((2 * NZ,)),
-            dma,
-            dma,
-            dma((NXH * NY,)),
-            dma((NXH * NY,)),
+            dma,
+            dma,
+            dma,
+            dma,
+            dma,
+            dma,
             pltpu.SemaphoreType.REGULAR,
             pltpu.SemaphoreType.REGULAR,
         ],

time: 30.7 us -> 27.4 us (0.89)
  the two profiles are of different devices: /device:TPU:64 before, /device:TPU:8 now
where the time goes in v2:
time: 27.4 us; the launch traced here: 27.3 us
  Pallas kernels  25.8 us (94%)
  between operations  0.66 us (2%)
  local copies, waits for them, and re-layouts  0.6 us (2%)
    pallas_call x1, Pallas kernels, attend(): pl.pallas_call(functools.partial(kernel, place // NX, place % NX), out_sh...  25.8 us
    unnamed x1, local copies, waits for them, and re-layouts  0.6 us

profile of v2, /device:TPU:8, one launch (start us, length us, event | category | flops | bytes accessed | tf_op | source)
XLA Modules:
  0.0 27.3 jit_solution(11430368098175485938)
XLA Ops:
  0.7 26.0 %conditional.1 = (bf16[8,512]{1,0:T(8,128)(2,1)S(1)}) conditional(s32[]{:T(128)} %bitcast, (s32[8]{0:T(128)}, s32[1,64]{1,0:T(1,128)}, s32[32]{0:T(128)}, s32[16]{0:T(128)}, bf16[8,1024]{1,0:T(8,128)(2,1)}, /*index=5*/bf16[2,2048,128]{2,1,0:T(8,128)(2,1)}, bf16[2,64,64,128]{3,2,1,0:T(8,128)(2,1)}, ...), branch_computations={%region_0.0_spmd, %region_1.0_spmd, %region_2.0_spmd, %region_3.0_... | conditional | bytes 8 | solution.py:429
  0.7 25.8 %attend_6.1 = bf16[8,512]{1,0:T(8,128)(2,1)S(1)} custom-call(s32[8]{0:T(128)} %get-tuple-element.326.lens_hbm, s32[1,64]{1,0:T(1,128)} %get-tuple-element.327.table_hbm, s32[32]{0:T(128)} %get-tuple-element.328.owner_hbm, s32[16]{0:T(128)} %get-tuple-element.329.readers_hbm, bf16[8,1024]{1,0:T(8,128)(2,1)} %get-tuple-element.330.q_hbm, ...), custom_call_target="tpu_custom_call" | custom-call | tf_op jit(solution)/shard_map/cond/branch_6_fun/attend_6/pallas_call | solution.py:383
  26.7 0.6 %copy.42 = bf16[8,512]{1,0:T(8,128)(2,1)} copy(bf16[8,512]{1,0:T(8,128)(2,1)S(1)} %get-tuple-element.406) | data formatting | bytes 16384

commit v3 on v2

--- a/solution.py
+++ b/solution.py
@@ -49,9 +49,7 @@
     w,
     q_buf,
     o_send,
-    s_send,
     o_recv,
-    s_recv,
     num_res,
     ml_res,
     attn_f32,
@@ -64,11 +62,10 @@
     q_send_sem,
     q_recv_sem,
     o_send_sem,
-    s_send_sem,
     o_recv_sem,
-    s_recv_sem,
     p_send_sem,
     p_recv_sem,
+    go,
     known,
     clear,
 ):
@@ -93,23 +90,25 @@
 
     barrier = pltpu.get_barrier_semaphore()
     beside = here == 1
+    elsewhere = jnp.logical_not(at_owner)
 
     def greet_tp(sem):
         for k in TP_STEPS:
             pl.semaphore_signal(sem, 1, device_id=tp_peer(*k), device_id_type=MESH)
 
+    pl.semaphore_signal(barrier, 1, device_id=at(z, x, 1 - c), device_id_type=MESH)
+
     @pl.when(at_owner)
     def _():
-        pl.semaphore_signal(barrier, 1, device_id=at(oz, ox, 1 - c), device_id_type=MESH)
         for i in range(2 * NZ - 1, 0, -1):
             pl.semaphore_signal(
                 barrier,
                 1,
-                device_id=at((oz + i // 2) % NZ, (ox + i % 2) % NX, c),
+                device_id=at((oz + i // 2) % NZ, (ox + i % 2) % NX, 0),
                 device_id_type=MESH,
             )
 
-    @pl.when(jnp.logical_not(at_owner))
+    @pl.when(jnp.logical_and(elsewhere, c == 1))
     def _():
         greet_tp(barrier)
 
@@ -168,44 +167,30 @@
             device_id_type=MESH,
         )
 
-    @pl.when(jnp.logical_not(at_owner))
-    def _():
+    @pl.when(jnp.logical_and(elsewhere, c == 0))
+    def _():
+        pl.semaphore_wait(barrier, NC + 1)
+        pl.semaphore_signal(go, 1, device_id=at(z, x, 1), device_id_type=MESH)
+        query_copy().start()
+
+    @pl.when(jnp.logical_and(elsewhere, c == 1))
+    def _():
+        pl.semaphore_wait(go, 1)
+        query_copy().start()
         pl.semaphore_wait(barrier, len(TP_STEPS) + 1)
-        query_copy().start()
+        greet_tp(known)
+        pl.semaphore_wait(known, len(TP_STEPS))
+        pl.semaphore_signal(clear, 1, device_id=at(z, x, 0), device_id_type=MESH)
 
         @pl.when(beside)
         def _():
-            greet_tp(known)
-            pl.semaphore_wait(known, len(TP_STEPS))
-            pl.semaphore_signal(clear, 1, device_id=at(oz, ox, c), device_id_type=MESH)
+            for core in range(NC):
+                pl.semaphore_signal(
+                    clear, 1, device_id=at(oz, ox, core), device_id_type=MESH
+                )
 
     for copy in load_scalars:
         copy.wait()
-    load_cache.wait()
-
-    def resident(b, carry):
-        mine = pl.ds(pl.multiple_of(b * heads, heads), heads)
-        keys = jnp.concatenate(
-            [cache[0, table_ref[0, b * per + j]] for j in range(per)], axis=0
-        )
-        s = nt_dot(q_f32[mine, :].astype(jnp.bfloat16), keys)
-        pos = lax.broadcasted_iota(jnp.int32, s.shape, 1)
-        s = jnp.where(pos < lens_ref[b], s, LOW)
-        m = jnp.max(s, axis=-1, keepdims=True)
-        e = jnp.exp2((s - m) * c2)
-        values = jnp.concatenate(
-            [cache[1, table_ref[0, b * per + j]] for j in range(per)], axis=0
-        )
-        ml_res[0, mine, :] = jnp.broadcast_to(m * c2, (heads, HD))
-        ml_res[1, mine, :] = jnp.broadcast_to(
-            jnp.sum(e, axis=-1, keepdims=True), (heads, HD)
-        )
-        num_res[mine, :] = jnp.dot(
-            e.astype(jnp.bfloat16), values, preferred_element_type=jnp.float32
-        )
-        return carry
-
-    lax.fori_loop(0, rows, resident, 0)
 
     @pl.when(at_owner)
     def _():
@@ -216,24 +201,13 @@
         source = (owner_ref[0] % NC + c) % 2
 
         def reply(i):
-            peer = at((oz + i // 2) % NZ, (ox + i % 2) % NX, c)
-            return (
-                pltpu.make_async_remote_copy(
-                    o_send.at[i],
-                    o_recv,
-                    o_send_sem,
-                    o_recv_sem,
-                    device_id=peer,
-                    device_id_type=MESH,
-                ),
-                pltpu.make_async_remote_copy(
-                    s_send.at[i],
-                    s_recv,
-                    s_send_sem,
-                    s_recv_sem,
-                    device_id=peer,
-                    device_id_type=MESH,
-                ),
+            return pltpu.make_async_remote_copy(
+                o_send.at[i],
+                o_recv,
+                o_send_sem,
+                o_recv_sem,
+                device_id=at((oz + i // 2) % NZ, (ox + i % 2) % NX, c),
+                device_id_type=MESH,
             )
 
         def arrival(i):
@@ -268,53 +242,79 @@
             )
             o = (num / total).astype(jnp.bfloat16)
             lse = jnp.broadcast_to(m * c2 + jnp.log(total) * LOG2E, (4 * n, HD))
+            line = lax.broadcasted_iota(jnp.int32, (8, HD), 0)
             for j in range(2):
                 row = jnp.transpose(lse[2 * n * j : 2 * n * (j + 1)])[0:8, :]
-                s_send[ids[2 * j]] = row
-                s_send[ids[2 * j + 1]] = row
-            for j in range(4):
-                o_send[ids[j]] = o[n * j : n * (j + 1)]
+                first = row.astype(jnp.bfloat16).astype(jnp.float32)
+                second = (row - first).astype(jnp.bfloat16).astype(jnp.float32)
+                terms = jnp.where(
+                    line == 0, first, jnp.where(line == 1, second, row - first - second)
+                )
+                terms = jnp.concatenate([terms, terms], axis=0).astype(jnp.bfloat16)
+                for k in range(2 * j, 2 * j + 2):
+                    o_send[ids[k], n:, :] = terms
+                    o_send[ids[k], 0:n, :] = o[n * k : n * (k + 1)]
             for i in ids[:0:-1]:
-                for copy in reply(i):
-                    copy.start()
+                reply(i).start()
 
             @pl.when(own == 0)
             def _():
-                for copy in reply(ids[0]):
-                    copy.start()
+                reply(ids[0]).start()
 
             return carry
 
         lax.fori_loop(0, NZ // 2, serve, 0)
         o_recv[...] = o_send[0]
-        s_recv[...] = s_send[0]
-        for ref, sem in ((o_send, o_send_sem), (s_send, s_send_sem)):
-            sent = ref.at[pl.ds(1, 2 * NZ - 1)]
-            pltpu.make_async_remote_copy(
-                sent, sent, sem, sem, device_id=at(oz, ox, 1 - c), device_id_type=MESH
-            ).wait_send()
-        pl.semaphore_wait(clear, 1)
-
-    @pl.when(jnp.logical_not(at_owner))
+        sent = o_send.at[pl.ds(1, 2 * NZ - 1)]
+        pltpu.make_async_remote_copy(
+            sent, sent, o_send_sem, o_recv_sem, device_id=at(oz, ox, 1 - c), device_id_type=MESH
+        ).wait_send()
+
+    load_cache.wait()
+
+    def resident(b, carry):
+        mine = pl.ds(pl.multiple_of(b * heads, heads), heads)
+        keys = jnp.concatenate(
+            [cache[0, table_ref[0, b * per + j]] for j in range(per)], axis=0
+        )
+        s = nt_dot(q_f32[mine, :].astype(jnp.bfloat16), keys)
+        pos = lax.broadcasted_iota(jnp.int32, s.shape, 1)
+        s = jnp.where(pos < lens_ref[b], s, LOW)
+        m = jnp.max(s, axis=-1, keepdims=True)
+        e = jnp.exp2((s - m) * c2)
+        values = jnp.concatenate(
+            [cache[1, table_ref[0, b * per + j]] for j in range(per)], axis=0
+        )
+        ml_res[0, mine, :] = jnp.broadcast_to(m * c2, (heads, HD))
+        ml_res[1, mine, :] = jnp.broadcast_to(
+            jnp.sum(e, axis=-1, keepdims=True), (heads, HD)
+        )
+        num_res[mine, :] = jnp.dot(
+            e.astype(jnp.bfloat16), values, preferred_element_type=jnp.float32
+        )
+        return carry
+
+    lax.fori_loop(0, rows, resident, 0)
+
+    @pl.when(elsewhere)
     def _():
         query_copy().wait_send()
         pltpu.make_async_remote_copy(
             o_recv, o_recv, o_send_sem, o_recv_sem, device_id=at(oz, ox, c), device_id_type=MESH
         ).wait_recv()
-        pltpu.make_async_remote_copy(
-            s_recv, s_recv, s_send_sem, s_recv_sem, device_id=at(oz, ox, c), device_id_type=MESH
-        ).wait_recv()
 
     reads = readers_ref[0] == dp
     for i in range(1, readers_ref.shape[0]):
         reads = jnp.logical_or(reads, readers_ref[i] == dp)
-    lse_f32[...] = jnp.transpose(jnp.broadcast_to(s_recv[0:1, :], (HD, HD)))
+    terms = o_recv[n:, :].astype(jnp.float32)
+    row = terms[0:1] + terms[1:2] + terms[2:3]
+    lse_f32[...] = jnp.transpose(jnp.broadcast_to(row, (HD, HD)))
     lse = lse_f32[pl.ds(pl.multiple_of(dx * n, n), n), :]
     lse = jnp.where(reads, lse, LOW)
     m_res, l_res = ml_res[0], ml_res[1]
     top = jnp.maximum(m_res, lse)
     w_res, w_pre = jnp.exp2(m_res - top), jnp.exp2(lse - top)
-    attn_f32[...] = (num_res[...] * w_res + o_recv[...].astype(jnp.float32) * w_pre) / (
+    attn_f32[...] = (num_res[...] * w_res + o_recv[0:n, :].astype(jnp.float32) * w_pre) / (
         l_res * w_res + w_pre
     )
     attn = jnp.concatenate(
@@ -323,14 +323,6 @@
 
     load_w.wait()
     cols = out_ref.shape[1]
-
-    def block(kx, ky):
-        start = (((xh + kx) % NXH) * NY + (y + ky) % NY) * cols
-        return jnp.dot(
-            attn,
-            w[:, pl.ds(pl.multiple_of(start, cols), cols)],
-            preferred_element_type=jnp.float32,
-        )
 
     def part_copy(kx, ky):
         i = kx * NY + ky
@@ -343,18 +335,30 @@
             device_id_type=MESH,
         )
 
+    @pl.when(jnp.logical_or(at_owner, c == 0))
+    def _():
+        pl.semaphore_wait(clear, 1)
+
     def project(i, carry):
-        kx, ky = 1 - i // NY, (i + 2) % NY
-        k = kx * NY + ky
-        part_send[k] = block(kx, ky)
-
-        @pl.when(k > 0)
-        def _():
-            part_copy(kx, ky).start()
+        kx, pair = 1 - i // 2, (y // 2 + 1 + i % 2) % 2
+        start = (((xh + kx) % NXH) * NY + pair * 2) * cols
+        both = jnp.dot(
+            attn,
+            w[:, pl.ds(pl.multiple_of(start, 2 * cols), 2 * cols)],
+            preferred_element_type=jnp.float32,
+        )
+        for j in range(2):
+            ky = (pair * 2 + j + NY - y) % NY
+            k = kx * NY + ky
+            part_send[k] = both[:, j * cols : (j + 1) * cols]
+
+            @pl.when(k > 0)
+            def _(ky=ky):
+                part_copy(kx, ky).start()
 
         return carry
 
-    lax.fori_loop(0, NXH * NY, project, 0)
+    lax.fori_loop(0, NXH * NY // 2, project, 0)
     others = pl.ds(1, NXH * NY - 1)
     whole = pltpu.make_async_remote_copy(
         part_send.at[others],
@@ -394,10 +398,8 @@
             pltpu.VMEM((2, 2, keys, HD), bf16),
             pltpu.VMEM(w_out.shape, bf16),
             pltpu.VMEM((2 * NZ, n, HD), bf16),
-            pltpu.VMEM((2 * NZ, n, HD), bf16),
-            pltpu.VMEM((2 * NZ, 8, HD), f32),
-            pltpu.VMEM((n, HD), bf16),
-            pltpu.VMEM((8, HD), f32),
+            pltpu.VMEM((2 * NZ, n + 16, HD), bf16),
+            pltpu.VMEM((n + 16, HD), bf16),
             pltpu.VMEM((n, HD), f32),
             pltpu.VMEM((2, n, HD), f32),
             pltpu.VMEM((n, HD), f32),
@@ -413,8 +415,7 @@
             dma,
             dma,
             dma,
-            dma,
-            dma,
+            pltpu.SemaphoreType.REGULAR,
             pltpu.SemaphoreType.REGULAR,
             pltpu.SemaphoreType.REGULAR,
         ],

time: 27.4 us -> 25.9 us (0.945)
  the two profiles are of different devices: /device:TPU:8 before, /device:TPU:32 now
where the time goes in v3:
time: 25.9 us; the launch traced here: 25.4 us
  Pallas kernels  23.9 us (92%)
  between operations  0.66 us (3%)
  local copies, waits for them, and re-layouts  0.6 us (2%)
    pallas_call x1, Pallas kernels, attend(): pl.pallas_call(functools.partial(kernel, place // NX, place % NX), out_sh...  23.9 us
    unnamed x1, local copies, waits for them, and re-layouts  0.6 us

profile of v3, /device:TPU:32, one launch (start us, length us, event | category | flops | bytes accessed | tf_op | source)
XLA Modules:
  0.0 25.4 jit_solution(17170678112012605369)
XLA Ops:
  0.7 24.1 %conditional.1 = (bf16[8,512]{1,0:T(8,128)(2,1)S(1)}) conditional(s32[]{:T(128)} %bitcast, (s32[8]{0:T(128)}, s32[1,64]{1,0:T(1,128)}, s32[32]{0:T(128)}, s32[16]{0:T(128)}, bf16[8,1024]{1,0:T(8,128)(2,1)}, /*index=5*/bf16[2,2048,128]{2,1,0:T(8,128)(2,1)}, bf16[2,64,64,128]{3,2,1,0:T(8,128)(2,1)}, ...), branch_computations={%region_0.0_spmd, %region_1.0_spmd, %region_2.0_spmd, %region_3.0_... | conditional | bytes 8 | solution.py:430
  0.9 23.9 %attend_14.1 = bf16[8,512]{1,0:T(8,128)(2,1)S(1)} custom-call(s32[8]{0:T(128)} %get-tuple-element.390.lens_hbm, s32[1,64]{1,0:T(1,128)} %get-tuple-element.391.table_hbm, s32[32]{0:T(128)} %get-tuple-element.392.owner_hbm, s32[16]{0:T(128)} %get-tuple-element.393.readers_hbm, bf16[8,1024]{1,0:T(8,128)(2,1)} %get-tuple-element.394.q_hbm, ...), custom_call_target="tpu_custom_call" | custom-call | tf_op jit(solution)/shard_map/cond/branch_14_fun/attend_14/pallas_call | solution.py:387
  24.8 0.6 %copy.42 = bf16[8,512]{1,0:T(8,128)(2,1)} copy(bf16[8,512]{1,0:T(8,128)(2,1)S(1)} %get-tuple-element.406) | data formatting | bytes 16384

commit v4 on v3

--- a/solution.py
+++ b/solution.py
@@ -17,6 +17,8 @@
     [(kx, ky) for kx in range(NXH) for ky in range(NY) if kx or ky],
     key=lambda k: -(2 * k[0] + min(k[1], NY - k[1])),
 )
+
+PLACES = sorted(range(1, 2 * NZ), key=lambda i: -(min(i // 2, NZ - i // 2) + i % 2))
 
 
 def nt_dot(a, b):
@@ -100,15 +102,15 @@
 
     @pl.when(at_owner)
     def _():
-        for i in range(2 * NZ - 1, 0, -1):
+        for i in PLACES:
             pl.semaphore_signal(
                 barrier,
                 1,
-                device_id=at((oz + i // 2) % NZ, (ox + i % 2) % NX, 0),
+                device_id=at((oz + i // 2) % NZ, (ox + i % 2) % NX, 1),
                 device_id_type=MESH,
             )
 
-    @pl.when(jnp.logical_and(elsewhere, c == 1))
+    @pl.when(jnp.logical_and(elsewhere, c == 0))
     def _():
         greet_tp(barrier)
 
@@ -163,24 +165,28 @@
             q_buf.at[here],
             q_send_sem,
             q_recv_sem.at[here],
-            device_id=at(oz, ox, c),
+            device_id=at(oz, ox, 1 - c),
             device_id_type=MESH,
         )
 
+    @pl.when(at_owner)
+    def _():
+        query_copy().start()
+
+    @pl.when(jnp.logical_and(elsewhere, c == 1))
+    def _():
+        pl.semaphore_wait(barrier, NC + 1)
+        pl.semaphore_signal(go, 1, device_id=at(z, x, 0), device_id_type=MESH)
+        query_copy().start()
+
     @pl.when(jnp.logical_and(elsewhere, c == 0))
-    def _():
-        pl.semaphore_wait(barrier, NC + 1)
-        pl.semaphore_signal(go, 1, device_id=at(z, x, 1), device_id_type=MESH)
-        query_copy().start()
-
-    @pl.when(jnp.logical_and(elsewhere, c == 1))
     def _():
         pl.semaphore_wait(go, 1)
         query_copy().start()
         pl.semaphore_wait(barrier, len(TP_STEPS) + 1)
         greet_tp(known)
         pl.semaphore_wait(known, len(TP_STEPS))
-        pl.semaphore_signal(clear, 1, device_id=at(z, x, 0), device_id_type=MESH)
+        pl.semaphore_signal(clear, 1, device_id=at(z, x, 1), device_id_type=MESH)
 
         @pl.when(beside)
         def _():
@@ -194,7 +200,6 @@
 
     @pl.when(at_owner)
     def _():
-        q_buf[0] = q_rows[...]
         load_kv.wait()
         for i in range(2):
             kv_copy(i).wait()
@@ -206,7 +211,7 @@
                 o_recv,
                 o_send_sem,
                 o_recv_sem,
-                device_id=at((oz + i // 2) % NZ, (ox + i % 2) % NX, c),
+                device_id=at((oz + i // 2) % NZ, (ox + i % 2) % NX, 1 - c),
                 device_id_type=MESH,
             )
 
@@ -226,11 +231,7 @@
             zb = NZ - za - 4 * own
             ids = (za * 2, za * 2 + 1, zb * 2, zb * 2 + 1)
 
-            @pl.when(own == 0)
-            def _():
-                arrival(ids[0]).wait_recv()
-
-            for i in ids[1:]:
+            for i in ids:
                 arrival(i).wait_recv()
             q = jnp.concatenate([q_buf[i] for i in ids], axis=0)
             s = nt_dot(q, kv[source, 0])
@@ -254,20 +255,13 @@
                 for k in range(2 * j, 2 * j + 2):
                     o_send[ids[k], n:, :] = terms
                     o_send[ids[k], 0:n, :] = o[n * k : n * (k + 1)]
-            for i in ids[:0:-1]:
+            for i in ids[::-1]:
                 reply(i).start()
-
-            @pl.when(own == 0)
-            def _():
-                reply(ids[0]).start()
-
             return carry
 
         lax.fori_loop(0, NZ // 2, serve, 0)
-        o_recv[...] = o_send[0]
-        sent = o_send.at[pl.ds(1, 2 * NZ - 1)]
         pltpu.make_async_remote_copy(
-            sent, sent, o_send_sem, o_recv_sem, device_id=at(oz, ox, 1 - c), device_id_type=MESH
+            o_send, o_send, o_send_sem, o_recv_sem, device_id=at(oz, ox, 1 - c), device_id_type=MESH
         ).wait_send()
 
     load_cache.wait()
@@ -296,12 +290,10 @@
 
     lax.fori_loop(0, rows, resident, 0)
 
-    @pl.when(elsewhere)
-    def _():
-        query_copy().wait_send()
-        pltpu.make_async_remote_copy(
-            o_recv, o_recv, o_send_sem, o_recv_sem, device_id=at(oz, ox, c), device_id_type=MESH
-        ).wait_recv()
+    query_copy().wait_send()
+    pltpu.make_async_remote_copy(
+        o_recv, o_recv, o_send_sem, o_recv_sem, device_id=at(oz, ox, 1 - c), device_id_type=MESH
+    ).wait_recv()
 
     reads = readers_ref[0] == dp
     for i in range(1, readers_ref.shape[0]):
@@ -335,7 +327,7 @@
             device_id_type=MESH,
         )
 
-    @pl.when(jnp.logical_or(at_owner, c == 0))
+    @pl.when(jnp.logical_or(at_owner, c == 1))
     def _():
         pl.semaphore_wait(clear, 1)
 

time: 25.9 us -> 24.7 us (0.954)
  the two profiles are of different devices: /device:TPU:32 before, /device:TPU:64 now
where the time goes in v4:
time: 24.7 us; the launch traced here: 24.5 us
  Pallas kernels  23 us (93%)
  between operations  0.66 us (3%)
  local copies, waits for them, and re-layouts  0.6 us (2%)
    pallas_call x1, Pallas kernels, attend(): pl.pallas_call(functools.partial(kernel, place // NX, place % NX), out_sh...  23 us
    unnamed x1, local copies, waits for them, and re-layouts  0.6 us

profile of v4, /device:TPU:64, one launch (start us, length us, event | category | flops | bytes accessed | tf_op | source)
XLA Modules:
  0.0 24.5 jit_solution(1740585810676194046)
XLA Ops:
  0.7 23.2 %conditional.1 = (bf16[8,512]{1,0:T(8,128)(2,1)S(1)}) conditional(s32[]{:T(128)} %bitcast, (s32[8]{0:T(128)}, s32[1,64]{1,0:T(1,128)}, s32[32]{0:T(128)}, s32[16]{0:T(128)}, bf16[8,1024]{1,0:T(8,128)(2,1)}, /*index=5*/bf16[2,2048,128]{2,1,0:T(8,128)(2,1)}, bf16[2,64,64,128]{3,2,1,0:T(8,128)(2,1)}, ...), branch_computations={%region_0.0_spmd, %region_1.0_spmd, %region_2.0_spmd, %region_3.0_... | conditional | bytes 8 | solution.py:422
  0.7 23.0 %attend_4.1 = bf16[8,512]{1,0:T(8,128)(2,1)S(1)} custom-call(s32[8]{0:T(128)} %get-tuple-element.310.lens_hbm, s32[1,64]{1,0:T(1,128)} %get-tuple-element.311.table_hbm, s32[32]{0:T(128)} %get-tuple-element.312.owner_hbm, s32[16]{0:T(128)} %get-tuple-element.313.readers_hbm, bf16[8,1024]{1,0:T(8,128)(2,1)} %get-tuple-element.314.q_hbm, ...), custom_call_target="tpu_custom_call" | custom-call | tf_op jit(solution)/shard_map/cond/branch_4_fun/attend_4/pallas_call | solution.py:379
  23.9 0.6 %copy.42 = bf16[8,512]{1,0:T(8,128)(2,1)} copy(bf16[8,512]{1,0:T(8,128)(2,1)S(1)} %get-tuple-element.406) | data formatting | bytes 16384
